TPU v7x, 32 devices: a whole 2x2x4 slice. The times are simulated.
32 devices in a mesh: dp: 8 (over z, x), tensor: 4 (over y, core).
Axes of the slice: x: 2, y: 2, z: 4, core: 2. Of those that a mesh axis runs over, the one named last changes fastest.
Arguments:
- tokens: bfloat16 [8192, 2048], P('dp'), may hold values from -6 to 6
- w_query: bfloat16 [2048, 2048], P('dp', 'tensor'), may hold values from -0.125 to 0.125
- w_key: bfloat16 [2048, 2048], P('dp', 'tensor'), may hold values from -0.125 to 0.125
- w_value: bfloat16 [2048, 4096], P('dp', 'tensor'), may hold values from -0.125 to 0.125
- w_gate: bfloat16 [2048, 4096], P('dp', 'tensor'), may hold values from -0.125 to 0.125
- w_out: bfloat16 [4096, 2048], P('tensor', 'dp'), may hold values from -0.125 to 0.125
- w_ffgate: bfloat16 [2048, 4096], P('dp', 'tensor'), may hold values from -0.125 to 0.125
- w_ffup: bfloat16 [2048, 4096], P('dp', 'tensor'), may hold values from -0.125 to 0.125
- w_down: bfloat16 [4096, 2048], P('tensor', 'dp'), may hold values from -0.125 to 0.125
- norm1_gain: bfloat16 [2048], P('dp'), may hold values from 0.5 to 1.5
- norm1_shift: bfloat16 [2048], P('dp'), may hold values from -1 to 1
- norm2_gain: bfloat16 [2048], P('dp'), may hold values from 0.5 to 1.5
- norm2_shift: bfloat16 [2048], P('dp'), may hold values from -1 to 1
- segment_ids: int32 [8192], P('dp'), may hold values from 0 to 63, never falling along the last dimension, each value on 1 to 512 neighbouring positions
- decay_index: int32 [8], P('tensor'), may hold values from 0 to 4
- cotangent: bfloat16 [8192, 2048], P('dp'), may hold values from -6 to 6
Outputs:
- block_out: bfloat16 [8192, 2048], P('dp')
- grad_tokens: float32 [8192, 2048], P('dp')
- grad_query: float32 [2048, 2048], P('dp', 'tensor')
- grad_key: float32 [2048, 2048], P('dp', 'tensor')
- grad_value: float32 [2048, 4096], P('dp', 'tensor')
- grad_gate: float32 [2048, 4096], P('dp', 'tensor')
- grad_out: float32 [4096, 2048], P('tensor', 'dp')
- grad_ffgate: float32 [2048, 4096], P('dp', 'tensor')
- grad_ffup: float32 [2048, 4096], P('dp', 'tensor')
- grad_down: float32 [4096, 2048], P('tensor', 'dp')
- grad_gain_one: float32 [2048], P('dp')
- grad_shift_one: float32 [2048], P('dp')
- grad_gain_two: float32 [2048], P('dp')
- grad_shift_two: float32 [2048], P('dp')
Inputs may be any that keep to these rules, and one draw needn't show every extreme that they name: `segment_ids`: segment numbers never fall along the tokens; a sequence boundary resets retention even where the number continues.
All inputs are finite; a program needn't handle non-finite values.
Results may differ from a plain program's by a relative error of at most 0.018.
Values may be sent and summed in bfloat16 or wider, within the bound.
No kernel may reach another device: no remote copies, remote signals or barrier semaphores. Data moves between devices by JAX's collectives and lax.ppermute only.
A program may use at most 256 MiB of HBM per device.

v0:
```python
import math
import jax
import jax.numpy as jnp
from jax import lax
from jax.sharding import PartitionSpec as P

HEAD_KEY = 256
HEAD_VALUE = 512
LENGTH = 1024
EPSILON = 1e-05
GROUP_EPSILON = 1.0
XPOS_SPAN = 512.0
INV_ROOT2 = 1.0 / math.sqrt(2.0)
INV_ROOT_TWO_PI = 1.0 / math.sqrt(2.0 * math.pi)


def xpos_tables(length, width):
    half = width // 2
    index = jnp.arange(half, dtype=jnp.float32)
    theta = jnp.exp(index * (-math.log(10000.0) / half))
    zeta = (2.0 * index + 0.4 * width) / (1.4 * width)
    position = jnp.arange(length, dtype=jnp.float32) - float(length // 2)
    angle = position[:, None] * theta[None, :]
    growth = jnp.exp(position[:, None] * (1.0 / XPOS_SPAN) * jnp.log(zeta)[None, :])
    return (jnp.cos(angle), jnp.sin(angle), growth)


def rotate(values, cosine, sine, factor):
    half = values.shape[-1] // 2
    first = values[..., :half]
    second = values[..., half:]
    cos_b = cosine[:, None, :]
    sin_b = sine[:, None, :]
    scale = factor[:, None, :]
    return jnp.concatenate(
        [(first * cos_b - second * sin_b) * scale, (second * cos_b + first * sin_b) * scale],
        axis=-1,
    )


def unrotate(grads, cosine, sine, factor):
    half = grads.shape[-1] // 2
    scale = factor[:, None, :]
    first = grads[..., :half] * scale
    second = grads[..., half:] * scale
    cos_b = cosine[:, None, :]
    sin_b = sine[:, None, :]
    return jnp.concatenate(
        [first * cos_b + second * sin_b, second * cos_b - first * sin_b], axis=-1
    )


def decay_mask(row_start, row_segment, col_segment, log_gamma):
    row_pos = row_start + jnp.arange(row_segment.shape[0], dtype=jnp.int32)
    col_pos = jnp.arange(col_segment.shape[0], dtype=jnp.int32)
    gap = row_pos[:, None] - col_pos[None, :]
    keep = (gap >= 0) & (row_segment[:, None] == col_segment[None, :])
    distance = jnp.maximum(gap, 0).astype(jnp.float32)
    return jnp.where(keep[None], jnp.exp(distance[None] * log_gamma[:, None, None]), 0.0)


def norm_parts(values, offset):
    centred = values - jnp.mean(values, axis=-1, keepdims=True)
    inv_scale = lax.rsqrt(jnp.mean(centred * centred, axis=-1, keepdims=True) + offset)
    return (centred * inv_scale, inv_scale)


def norm_back(grad_out, normed, inv_scale, gain):
    grad_norm = grad_out * gain
    return inv_scale * (
        grad_norm
        - jnp.mean(grad_norm, axis=-1, keepdims=True)
        - normed * jnp.mean(grad_norm * normed, axis=-1, keepdims=True)
    )


def retention_forward(query_rot, key_rot, values, segment, log_gamma):
    length = query_rot.shape[0]
    rows = min(512, length)
    outputs = []
    for block_start in range(0, length, rows):
        raw = jnp.einsum(
            "nhk,mhk->hnm",
            query_rot[block_start : block_start + rows],
            key_rot,
            preferred_element_type=jnp.float32,
        )
        mask = decay_mask(
            block_start, segment[block_start : block_start + rows], segment, log_gamma
        )
        weighted = (raw * mask).astype(jnp.bfloat16)
        outputs.append(
            jnp.einsum("hnm,mhv->nhv", weighted, values, preferred_element_type=jnp.float32)
        )
    return jnp.concatenate(outputs, axis=0)


def retention_backward(query_rot, key_rot, values, segment, log_gamma, grad_mixed):
    length = query_rot.shape[0]
    rows = min(512, length)
    grad_query = []
    grad_key = jnp.zeros(key_rot.shape, jnp.float32)
    grad_value = jnp.zeros(values.shape, jnp.float32)
    for block_start in range(0, length, rows):
        query_block = query_rot[block_start : block_start + rows]
        grad_block = grad_mixed[block_start : block_start + rows]
        raw = jnp.einsum("nhk,mhk->hnm", query_block, key_rot, preferred_element_type=jnp.float32)
        mask = decay_mask(
            block_start, segment[block_start : block_start + rows], segment, log_gamma
        )
        weighted = (raw * mask).astype(jnp.bfloat16)
        grad_value = grad_value + jnp.einsum(
            "hnm,nhv->mhv", weighted, grad_block, preferred_element_type=jnp.float32
        )
        grad_weighted = jnp.einsum(
            "nhv,mhv->hnm", grad_block, values, preferred_element_type=jnp.float32
        )
        grad_raw = (grad_weighted * mask).astype(jnp.bfloat16)
        grad_query.append(
            jnp.einsum("hnm,mhk->nhk", grad_raw, key_rot, preferred_element_type=jnp.float32)
        )
        grad_key = grad_key + jnp.einsum(
            "hnm,nhk->mhk", grad_raw, query_block, preferred_element_type=jnp.float32
        )
    return (jnp.concatenate(grad_query, axis=0), grad_key, grad_value)


def dense(left, right):
    return jnp.dot(left, right, preferred_element_type=jnp.float32)


def local(
    tokens,
    w_query,
    w_key,
    w_value,
    w_gate,
    w_out,
    w_ffgate,
    w_ffup,
    w_down,
    norm1_gain,
    norm1_shift,
    norm2_gain,
    norm2_shift,
    segment_ids,
    decay_index,
    cotangent,
):
    gathered = (
        lax.all_gather(w_query, "dp", axis=0, tiled=True),
        lax.all_gather(w_key, "dp", axis=0, tiled=True),
        lax.all_gather(w_value, "dp", axis=0, tiled=True),
        lax.all_gather(w_gate, "dp", axis=0, tiled=True),
        lax.all_gather(w_out, "dp", axis=1, tiled=True),
        lax.all_gather(w_ffgate, "dp", axis=0, tiled=True),
        lax.all_gather(w_ffup, "dp", axis=0, tiled=True),
        lax.all_gather(w_down, "dp", axis=1, tiled=True),
        lax.all_gather(norm1_gain, "dp", axis=0, tiled=True),
        lax.all_gather(norm1_shift, "dp", axis=0, tiled=True),
        lax.all_gather(norm2_gain, "dp", axis=0, tiled=True),
        lax.all_gather(norm2_shift, "dp", axis=0, tiled=True),
    )
    (
        full_query,
        full_key,
        full_value,
        full_gate,
        full_out,
        full_ffgate,
        full_ffup,
        full_down,
        gain_one,
        shift_one,
        gain_two,
        shift_two,
    ) = gathered
    count = tokens.shape[0]
    seqs = count // LENGTH
    heads = full_query.shape[1] // HEAD_KEY
    inputs = tokens.astype(jnp.float32)
    log_gamma = jnp.log1p(-jnp.exp2(-5.0 - decay_index.astype(jnp.float32)))
    normed_one, scale_one = norm_parts(inputs, EPSILON)
    first_in = (normed_one * gain_one.astype(jnp.float32) + shift_one.astype(jnp.float32)).astype(
        jnp.bfloat16
    )
    query = dense(first_in, full_query).reshape(seqs, LENGTH, heads, HEAD_KEY)
    keys = dense(first_in, full_key).reshape(seqs, LENGTH, heads, HEAD_KEY)
    values_seq = (
        dense(first_in, full_value).astype(jnp.bfloat16).reshape(seqs, LENGTH, heads, HEAD_VALUE)
    )
    gate = dense(first_in, full_gate)
    cosine, sine, growth = xpos_tables(LENGTH, HEAD_KEY)
    query_rot = rotate(query, cosine, sine, growth).astype(jnp.bfloat16)
    key_rot = (rotate(keys, cosine, sine, 1.0 / growth) * HEAD_KEY ** (-0.5)).astype(jnp.bfloat16)
    segments = segment_ids.reshape(seqs, LENGTH)
    mixed = lax.map(
        lambda item: retention_forward(item[0], item[1], item[2], item[3], log_gamma),
        (query_rot, key_rot, values_seq, segments),
    )
    grouped, group_scale = norm_parts(mixed.reshape(count, heads, HEAD_VALUE), GROUP_EPSILON)
    grouped_flat = grouped.reshape(count, heads * HEAD_VALUE)
    sigmoid_gate = jax.nn.sigmoid(gate)
    swish = gate * sigmoid_gate
    gated = (swish * grouped_flat).astype(jnp.bfloat16)
    attention = lax.psum(dense(gated, full_out), "tensor")
    middle = inputs + attention
    normed_two, scale_two = norm_parts(middle, EPSILON)
    second_in = (normed_two * gain_two.astype(jnp.float32) + shift_two.astype(jnp.float32)).astype(
        jnp.bfloat16
    )
    ff_gate = dense(second_in, full_ffgate)
    ff_up = dense(second_in, full_ffup)
    normal_cdf = 0.5 * (1.0 + lax.erf(ff_gate * INV_ROOT2))
    activation = ff_gate * normal_cdf
    hidden = (activation * ff_up).astype(jnp.bfloat16)
    feed = lax.psum(dense(hidden, full_down).astype(jnp.bfloat16), "tensor").astype(jnp.float32)
    block_out = (middle + feed).astype(jnp.bfloat16)
    again = (
        lax.all_gather(w_query, "dp", axis=0, tiled=True),
        lax.all_gather(w_key, "dp", axis=0, tiled=True),
        lax.all_gather(w_value, "dp", axis=0, tiled=True),
        lax.all_gather(w_gate, "dp", axis=0, tiled=True),
        lax.all_gather(w_out, "dp", axis=1, tiled=True),
        lax.all_gather(w_ffgate, "dp", axis=0, tiled=True),
        lax.all_gather(w_ffup, "dp", axis=0, tiled=True),
        lax.all_gather(w_down, "dp", axis=1, tiled=True),
        lax.all_gather(norm1_gain, "dp", axis=0, tiled=True),
        lax.all_gather(norm1_shift, "dp", axis=0, tiled=True),
        lax.all_gather(norm2_gain, "dp", axis=0, tiled=True),
        lax.all_gather(norm2_shift, "dp", axis=0, tiled=True),
    )
    (
        back_query,
        back_key,
        back_value,
        back_gate,
        back_out,
        back_ffgate,
        back_ffup,
        back_down,
        back_gain_one,
        back_shift_one,
        back_gain_two,
        back_shift_two,
    ) = again
    grad_result = cotangent.astype(jnp.float32)
    grad_feed = grad_result.astype(jnp.bfloat16)
    grad_down = dense(hidden.T, grad_feed)
    grad_hidden = dense(grad_feed, back_down.T)
    density = jnp.exp(-0.5 * ff_gate * ff_gate) * INV_ROOT_TWO_PI
    grad_ffgate_in = (grad_hidden * ff_up * (normal_cdf + ff_gate * density)).astype(jnp.bfloat16)
    grad_ffup_in = (grad_hidden * activation).astype(jnp.bfloat16)
    grad_ffgate = dense(second_in.T, grad_ffgate_in)
    grad_ffup = dense(second_in.T, grad_ffup_in)
    grad_second = lax.psum(
        dense(grad_ffgate_in, back_ffgate.T) + dense(grad_ffup_in, back_ffup.T), "tensor"
    )
    grad_gain_two = jnp.sum(grad_second * normed_two, axis=0)
    grad_shift_two = jnp.sum(grad_second, axis=0)
    grad_middle = grad_result + norm_back(
        grad_second, normed_two, scale_two, back_gain_two.astype(jnp.float32)
    )
    grad_branch = grad_middle.astype(jnp.bfloat16)
    grad_out = dense(gated.T, grad_branch)
    grad_gated = dense(grad_branch, back_out.T)
    swish_slope = sigmoid_gate * (1.0 + gate * (1.0 - sigmoid_gate))
    grad_gate_in = (grad_gated * grouped_flat * swish_slope).astype(jnp.bfloat16)
    grad_grouped = (grad_gated * swish).reshape(count, heads, HEAD_VALUE)
    grad_mixed = norm_back(grad_grouped, grouped, group_scale, 1.0).astype(jnp.bfloat16)
    grad_mixed_seq = grad_mixed.reshape(seqs, LENGTH, heads, HEAD_VALUE)
    grad_qrot, grad_krot, grad_values = lax.map(
        lambda item: retention_backward(item[0], item[1], item[2], item[3], log_gamma, item[4]),
        (query_rot, key_rot, values_seq, segments, grad_mixed_seq),
    )
    grad_query_in = (
        unrotate(grad_qrot, cosine, sine, growth)
        .astype(jnp.bfloat16)
        .reshape(count, heads * HEAD_KEY)
    )
    grad_key_in = (
        (unrotate(grad_krot, cosine, sine, 1.0 / growth) * HEAD_KEY ** (-0.5))
        .astype(jnp.bfloat16)
        .reshape(count, heads * HEAD_KEY)
    )
    grad_value_in = grad_values.astype(jnp.bfloat16).reshape(count, heads * HEAD_VALUE)
    grad_query = dense(first_in.T, grad_query_in)
    grad_key = dense(first_in.T, grad_key_in)
    grad_value = dense(first_in.T, grad_value_in)
    grad_gate = dense(first_in.T, grad_gate_in)
    partial_first = (
        dense(grad_query_in, back_query.T)
        + dense(grad_key_in, back_key.T)
        + dense(grad_value_in, back_value.T)
        + dense(grad_gate_in, back_gate.T)
    )
    grad_first = lax.psum(partial_first.astype(jnp.bfloat16), "tensor").astype(jnp.float32)
    grad_gain_one = jnp.sum(grad_first * normed_one, axis=0)
    grad_shift_one = jnp.sum(grad_first, axis=0)
    grad_tokens = grad_middle + norm_back(
        grad_first, normed_one, scale_one, back_gain_one.astype(jnp.float32)
    )
    shares = tuple(
        (
            lax.psum_scatter(grad_query, "dp", scatter_dimension=0, tiled=True),
            lax.psum_scatter(grad_key, "dp", scatter_dimension=0, tiled=True),
            lax.psum_scatter(grad_value, "dp", scatter_dimension=0, tiled=True),
            lax.psum_scatter(grad_gate, "dp", scatter_dimension=0, tiled=True),
            lax.psum_scatter(grad_out, "dp", scatter_dimension=1, tiled=True),
            lax.psum_scatter(grad_ffgate, "dp", scatter_dimension=0, tiled=True),
            lax.psum_scatter(grad_ffup, "dp", scatter_dimension=0, tiled=True),
            lax.psum_scatter(grad_down, "dp", scatter_dimension=1, tiled=True),
            lax.psum_scatter(grad_gain_one, "dp", scatter_dimension=0, tiled=True),
            lax.psum_scatter(grad_shift_one, "dp", scatter_dimension=0, tiled=True),
            lax.psum_scatter(grad_gain_two, "dp", scatter_dimension=0, tiled=True),
            lax.psum_scatter(grad_shift_two, "dp", scatter_dimension=0, tiled=True),
        )
    )
    return (block_out, grad_tokens) + shares


def solution(mesh):
    placed = (
        P("dp", None),
        P("dp", "tensor"),
        P("dp", "tensor"),
        P("dp", "tensor"),
        P("dp", "tensor"),
        P("tensor", "dp"),
        P("dp", "tensor"),
        P("dp", "tensor"),
        P("tensor", "dp"),
        P("dp"),
        P("dp"),
        P("dp"),
        P("dp"),
        P("dp"),
        P("tensor"),
        P("dp", None),
    )
    return jax.shard_map(
        local,
        mesh=mesh,
        in_specs=placed,
        out_specs=(
            P("dp", None),
            P("dp", None),
            P("dp", "tensor"),
            P("dp", "tensor"),
            P("dp", "tensor"),
            P("dp", "tensor"),
            P("tensor", "dp"),
            P("dp", "tensor"),
            P("dp", "tensor"),
            P("tensor", "dp"),
            P("dp"),
            P("dp"),
            P("dp"),
            P("dp"),
        ),
        check_vma=False,
    )
```

profile of v0, /device:TPU:0, one launch (start us, length us, event | category | flops | bytes accessed | tf_op | source)
XLA Modules:
  0.0 2234.8 jit_solution(5405685063912232103)
XLA Ops:
  12.3 3.2 convert_reduce_fusion.1
  19.0 22.3 all-gather
  41.4 16.7 all-gather.1
  61.8 3.7 fusion.8
  65.5 5.2 fusion.59
  76.4 35.5 %all-gather.19.cloned.1.call-done = bf16[2048,512]{1,0:T(8,128)(2,1)} async-done(((bf16[256,512]{1,0:T(8,128)(2,1)}), bf16[2048,512]{1,0:T(8,128)(2,1)}) %all-gather.19.cloned.1.call-update) | async-done | bytes 2097168 | tf_op jit(solution)/shard_map/all_gather | solution.py:152
  111.9 5.2 fusion.60
  118.7 2.6 copy.126
  121.3 2.6 copy.127
  124.0 2.7 multiply_convert_fusion.9
  126.9 2.6 multiply_convert_fusion.6
  129.5 2.6 multiply_convert_fusion.7
  132.1 53.3 %all-gather.15.cloned.1.call-done = bf16[2048,1024]{1,0:T(8,128)(2,1)} async-done(((bf16[256,1024]{1,0:T(8,128)(2,1)}), bf16[2048,1024]{1,0:T(8,128)(2,1)}) %all-gather.15.cloned.1.call-update) | async-done | bytes 4194320 | tf_op jit(solution)/shard_map/all_gather | solution.py:153
  185.4 8.4 convolution_convert_fusion.1
  198.9 59.9 %all-gather.13.cloned.1.call-done = bf16[2048,1024]{1,0:T(8,128)(2,1)} async-done(((bf16[256,1024]{1,0:T(8,128)(2,1)}), bf16[2048,1024]{1,0:T(8,128)(2,1)}) %all-gather.13.cloned.1.call-update) | async-done | bytes 4194320 | tf_op jit(solution)/shard_map/all_gather | solution.py:154
  258.8 12.2 multiply_convert_fusion.5
  271.0 62.9 %all-gather.21.cloned.1.call-done = bf16[1024,2048]{1,0:T(8,128)(2,1)} async-done(((bf16[1024,256]{1,0:T(8,128)(2,1)}), bf16[1024,2048]{1,0:T(8,128)(2,1)}) %all-gather.21.cloned.1.call-update) | async-done | bytes 4194320 | tf_op jit(solution)/shard_map/all_gather | solution.py:155
  333.9 11.0 fusion.63
  347.2 17.7 all-gather.2
  365.0 16.9 all-gather.3
  381.9 114.3 %all-reduce.10.cloned.1.call-done = f32[1024,2048]{1,0:T(8,128)} async-done(((f32[1024,2048]{1,0:T(8,128)}), f32[1024,2048]{1,0:T(8,128)}) %all-reduce.10.cloned.1.call-update) | async-done | bytes 8388624 | tf_op jit(solution)/shard_map/psum | solution.py:206
  496.1 5.5 fusion.55
  505.0 3.0 add_convert_fusion.2
  508.0 63.2 %all-gather.23.cloned.1.call-done = bf16[2048,1024]{1,0:T(8,128)(2,1)} async-done(((bf16[256,1024]{1,0:T(8,128)(2,1)}), bf16[2048,1024]{1,0:T(8,128)(2,1)}) %all-gather.23.cloned.1.call-update) | async-done | bytes 4194320 | tf_op jit(solution)/shard_map/all_gather | solution.py:156
  571.2 10.0 fusion.64
  581.2 63.5 %all-gather.25.cloned.1.call-done = bf16[2048,1024]{1,0:T(8,128)(2,1)} async-done(((bf16[256,1024]{1,0:T(8,128)(2,1)}), bf16[2048,1024]{1,0:T(8,128)(2,1)}) %all-gather.25.cloned.1.call-update) | async-done | bytes 4194320 | tf_op jit(solution)/shard_map/all_gather | solution.py:157
  644.7 10.0 fusion.65
  654.7 65.2 %all-gather.27.cloned.1.call-done = bf16[1024,2048]{1,0:T(8,128)(2,1)} async-done(((bf16[1024,256]{1,0:T(8,128)(2,1)}), bf16[1024,2048]{1,0:T(8,128)(2,1)}) %all-gather.27.cloned.1.call-update) | async-done | bytes 4194320 | tf_op jit(solution)/shard_map/all_gather | solution.py:158
  719.9 12.7 multiply_convert_fusion.3
  732.7 4.6 fusion.66
  737.3 6.9 convolution_add_fusion
  744.5 9.4 convolution_convert_fusion
  753.9 141.5 %all-reduce.12.cloned.1.call-done = f32[1024,2048]{1,0:T(8,128)} async-done(((f32[1024,2048]{1,0:T(8,128)}), f32[1024,2048]{1,0:T(8,128)}) %all-reduce.12.cloned.1.call-update) | async-done | bytes 8388624 | tf_op jit(solution)/shard_map/psum | solution.py:256
  895.5 8.3 multiply_reduce_fusion
  903.8 7.5 multiply_add_fusion
  911.5 13.1 multiply_convert_fusion
  924.6 3.5 bitcast_reduce_fusion
  936.9 3.3 fusion.40
  949.1 2.6 copy.103
  951.8 4.2 add_convert_fusion.3
  959.0 6.9 fusion.68
  965.9 6.9 fusion.69
  972.7 11.4 add_convert_fusion
  984.4 6.7 fusion.71
  992.3 6.5 fusion.70
  1000.5 9.1 fusion.74
  1011.2 9.1 fusion.75
  1022.1 8.8 fusion.76
  1032.5 10.1 fusion.29
  1044.2 9.1 fusion.72
  1054.8 9.1 fusion.73
  1065.8 71.5 %all-reduce.14.cloned.1.call-done = (bf16[1024,2048]{1,0:T(8,128)(2,1)}, bf16[1024,2048]{1,0:T(8,128)(2,1)}) async-done(((bf16[1024,2048]{1,0:T(8,128)(2,1)}, bf16[1024,2048]{1,0:T(8,128)(2,1)}), (bf16[1024,2048]{1,0:T(8,128)(2,1)}, bf16[1024,2048]{1,0:T(8,128)(2,1)})) %all-reduce.14.cloned.1.call-update) | async-done | bytes 8388624 | tf_op jit(solution)/shard_map/psum | solution.py:217
  1137.3 6.2 fusion.14
  1143.6 39.5 %all-reduce.4 = (f32[2048]{0:T(1024)S(1)}, f32[2048]{0:T(1024)S(1)}, f32[2048]{0:T(1024)S(1)}, f32[2048]{0:T(1024)S(1)}) all-reduce(f32[2048]{0:T(1024)S(1)} %get-tuple-element.68, f32[2048]{0:T(1024)S(1)} %get-tuple-element.72, f32[2048]{0:T(1024)S(1)} %copy-done.48, ...), channel_id=10, replica_groups=mesh['dp'=8,'tensor'=4] {'dp'}, use_global_device_ids=true, to_apply=%region_25.26.clone | all-reduce | flops 8192 | bytes 65536
  1185.6 8.5 add_convert_fusion.1
  1194.1 7.4 fusion.11
  1201.5 28.9 %reduce-scatter.11.cloned.1.call-done = f32[256,512]{1,0:T(8,128)} async-done(((f32[2048,512]{1,0:T(8,128)}), f32[256,512]{1,0:T(8,128)}) %reduce-scatter.11.cloned.1.call-update) | async-done | bytes 524304 | tf_op jit(solution)/shard_map/reduce_scatter | solution.py:306
  1230.4 92.2 %reduce-scatter.9.cloned.1.call-done = f32[256,512]{1,0:T(8,128)} async-done(((f32[2048,512]{1,0:T(8,128)}), f32[256,512]{1,0:T(8,128)}) %reduce-scatter.9.cloned.1.call-update) | async-done | bytes 524304 | tf_op jit(solution)/shard_map/reduce_scatter | solution.py:305
  1322.6 151.2 %reduce-scatter.19.cloned.1.call-done = f32[256,1024]{1,0:T(8,128)} async-done(((f32[2048,1024]{1,0:T(8,128)}), f32[256,1024]{1,0:T(8,128)}) %reduce-scatter.19.cloned.1.call-update) | async-done | bytes 1048592 | tf_op jit(solution)/shard_map/reduce_scatter | solution.py:310
  1473.8 150.6 %reduce-scatter.21.cloned.1.call-done = f32[256,1024]{1,0:T(8,128)} async-done(((f32[2048,1024]{1,0:T(8,128)}), f32[256,1024]{1,0:T(8,128)}) %reduce-scatter.21.cloned.1.call-update) | async-done | bytes 1048592 | tf_op jit(solution)/shard_map/reduce_scatter | solution.py:311
  1624.4 151.0 %reduce-scatter.23.cloned.1.call-done = f32[1024,256]{1,0:T(8,128)} async-done(((f32[1024,2048]{1,0:T(8,128)}), f32[1024,256]{1,0:T(8,128)}) %reduce-scatter.23.cloned.1.call-update) | async-done | bytes 1048592 | tf_op jit(solution)/shard_map/reduce_scatter | solution.py:312
  1775.5 151.1 %reduce-scatter.17.cloned.1.call-done = f32[1024,256]{1,0:T(8,128)} async-done(((f32[1024,2048]{1,0:T(8,128)}), f32[1024,256]{1,0:T(8,128)}) %reduce-scatter.17.cloned.1.call-update) | async-done | bytes 1048592 | tf_op jit(solution)/shard_map/reduce_scatter | solution.py:309
  1926.5 150.7 %reduce-scatter.13.cloned.1.call-done = f32[256,1024]{1,0:T(8,128)} async-done(((f32[2048,1024]{1,0:T(8,128)}), f32[256,1024]{1,0:T(8,128)}) %reduce-scatter.13.cloned.1.call-update) | async-done | bytes 1048592 | tf_op jit(solution)/shard_map/reduce_scatter | solution.py:307
  2077.2 150.8 %reduce-scatter.15.cloned.1.call-done = f32[256,1024]{1,0:T(8,128)} async-done(((f32[2048,1024]{1,0:T(8,128)}), f32[256,1024]{1,0:T(8,128)}) %reduce-scatter.15.cloned.1.call-update) | async-done | bytes 1048592 | tf_op jit(solution)/shard_map/reduce_scatter | solution.py:308
  (235 shorter events, 66.1 us)
Async XLA Ops:
  7.2 58.3 %all-gather.17.cloned.1.call-start = ((), (), s32[]{:S(2)}) async-start(), calls=%async_computation.10 | async-start | bytes 2359296 | tf_op jit(solution)/shard_map/all_gather | solution.py:151
  7.9 104.0 %all-gather.19.cloned.1.call-start = ((), (), s32[]{:S(2)}) async-start(), calls=%async_computation.11 | async-start | bytes 2359296 | tf_op jit(solution)/shard_map/all_gather | solution.py:152
  8.7 176.8 %all-gather.15.cloned.1.call-start = ((), (), s32[]{:S(2)}) async-start(), calls=%async_computation.9 | async-start | bytes 4718592 | tf_op jit(solution)/shard_map/all_gather | solution.py:153
  9.4 249.4 %all-gather.13.cloned.1.call-start = ((), (), s32[]{:S(2)}) async-start(), calls=%async_computation.8 | async-start | bytes 4718592 | tf_op jit(solution)/shard_map/all_gather | solution.py:154
  10.0 323.9 %all-gather.21.cloned.1.call-start = ((), (), s32[]{:S(2)}) async-start(), calls=%async_computation.12 | async-start | bytes 4718592 | tf_op jit(solution)/shard_map/all_gather | solution.py:155
  10.6 485.6 %all-reduce.10.cloned.1.call-start = ((), (), s32[]{:S(2)}) async-start(), calls=%async_computation.13 | async-start | bytes 16777216 | tf_op jit(solution)/shard_map/psum | solution.py:206
  10.6 4.9 copy-start.1
  12.3 4.5 copy-start.50
  12.3 4.5 copy-start.55
  15.5 3.5 copy-start.56
  15.5 25.8 %copy-start.57 = (bf16[256]{0:T(256)(128)(2,1)S(1)}, bf16[256]{0:T(256)(128)(2,1)}, u32[]{:S(2)}) copy-start(bf16[256]{0:T(256)(128)(2,1)} %param.26) | copy-start | bytes 1540
  15.5 46.3 %copy-start.44 = (f32[1024]{0:T(1024)}, f32[1024]{0:T(1024)S(1)}, u32[]{:S(2)}) copy-start(f32[1024]{0:T(1024)S(1)} %broadcast_multiply_fusion.9) | copy-start | bytes 12292
  16.8 45.1 %copy-start.46 = (f32[1024]{0:T(1024)}, f32[1024]{0:T(1024)S(1)}, u32[]{:S(2)}) copy-start(f32[1024]{0:T(1024)S(1)} %add_rsqrt_fusion.2) | copy-start | bytes 12292
  17.0 106.9 %copy-start.14 = (f32[1024,128]{1,0:T(8,128)}, f32[1024,128]{1,0:T(8,128)S(1)}, u32[]{:S(2)}) copy-start(f32[1024,128]{1,0:T(8,128)S(1)} %get-tuple-element.103) | copy-start | bytes 1572868
  17.1 106.9 %copy-start.16 = (f32[1024,128]{1,0:T(8,128)}, f32[1024,128]{1,0:T(8,128)S(1)}, u32[]{:S(2)}) copy-start(f32[1024,128]{1,0:T(8,128)S(1)} %get-tuple-element.104) | copy-start | bytes 1572868
  19.0 105.0 %copy-start.18 = (f32[1024,128]{1,0:T(8,128)}, f32[1024,128]{1,0:T(8,128)S(1)}, u32[]{:S(2)}) copy-start(f32[1024,128]{1,0:T(8,128)S(1)} %get-tuple-element.105) | copy-start | bytes 1572868
  19.0 105.0 %copy-start.20 = (f32[1024,128]{1,0:T(8,128)}, f32[1024,128]{1,0:T(8,128)S(1)}, u32[]{:S(2)}) copy-start(f32[1024,128]{1,0:T(8,128)S(1)} %get-tuple-element.106) | copy-start | bytes 1572868
  41.3 20.5 copy-start.42
  123.9 2.9 copy-start.28
  124.0 2.9 copy-start.38
  126.6 2.8 copy-start.10
  126.7 2.8 copy-start.12
  126.9 2.6 copy-start.30
  126.9 2.6 copy-start.40
  185.4 8.4 copy-start.26
  193.8 3.7 copy-start.60
  344.9 20.1 copy-start.59
  344.9 226.3 %all-gather.23.cloned.1.call-start = ((), (), s32[]{:S(2)}) async-start(), calls=%async_computation.14 | async-start | bytes 4718592 | tf_op jit(solution)/shard_map/all_gather | solution.py:156
  345.7 299.0 %all-gather.25.cloned.1.call-start = ((), (), s32[]{:S(2)}) async-start(), calls=%async_computation.15 | async-start | bytes 4718592 | tf_op jit(solution)/shard_map/all_gather | solution.py:157
  346.4 373.5 %all-gather.27.cloned.1.call-start = ((), (), s32[]{:S(2)}) async-start(), calls=%async_computation.16 | async-start | bytes 4718592 | tf_op jit(solution)/shard_map/all_gather | solution.py:158
  347.1 548.3 %all-reduce.12.cloned.1.call-start = ((), (), s32[]{:S(2)}) async-start(), calls=%async_computation.17 | async-start | bytes 16777216 | tf_op jit(solution)/shard_map/psum | solution.py:256
  501.6 3.4 copy-start
  719.9 12.7 copy-start.52
  732.7 4.6 copy-start.66
  732.7 4.6 copy-start.64
  732.7 4.6 copy-start.53
  744.3 393.0 %all-reduce.14.cloned.1.call-start = ((), (), s32[]{:S(2)}) async-start(), calls=%async_computation.26 | async-start | bytes 16777216 | tf_op jit(solution)/shard_map/psum | solution.py:217
  895.5 8.3 copy-start.23
  903.8 7.5 copy-start.5
  903.8 7.7 copy-start.6
  911.3 13.2 copy-start.3
  930.5 6.4 copy-start.8
  944.2 7.6 copy-start.9
  951.8 4.3 copy-start.36
  951.8 4.3 copy-start.54
  956.0 2.4 copy-start.33
  956.1 2.9 copy-start.51
  959.0 6.9 copy-start.22
  959.0 6.9 copy-start.24
  984.1 246.3 %reduce-scatter.11.cloned.1.call-start = ((), (), s32[]{:S(2)}) async-start(), calls=%async_computation.19 | async-start | bytes 4718592 | tf_op jit(solution)/shard_map/reduce_scatter | solution.py:306
  991.1 331.5 %reduce-scatter.9.cloned.1.call-start = ((), (), s32[]{:S(2)}) async-start(), calls=%async_computation.18 | async-start | bytes 4718592 | tf_op jit(solution)/shard_map/reduce_scatter | solution.py:305
  998.9 474.9 %reduce-scatter.19.cloned.1.call-start = ((), (), s32[]{:S(2)}) async-start(), calls=%async_computation.23 | async-start | bytes 9437184 | tf_op jit(solution)/shard_map/reduce_scatter | solution.py:310
  1009.6 614.8 %reduce-scatter.21.cloned.1.call-start = ((), (), s32[]{:S(2)}) async-start(), calls=%async_computation.24 | async-start | bytes 9437184 | tf_op jit(solution)/shard_map/reduce_scatter | solution.py:311
  1020.4 755.1 %reduce-scatter.23.cloned.1.call-start = ((), (), s32[]{:S(2)}) async-start(), calls=%async_computation.25 | async-start | bytes 9437184 | tf_op jit(solution)/shard_map/reduce_scatter | solution.py:312
  1030.9 895.6 %reduce-scatter.17.cloned.1.call-start = ((), (), s32[]{:S(2)}) async-start(), calls=%async_computation.22 | async-start | bytes 9437184 | tf_op jit(solution)/shard_map/reduce_scatter | solution.py:309
  1042.6 1034.6 %reduce-scatter.13.cloned.1.call-start = ((), (), s32[]{:S(2)}) async-start(), calls=%async_computation.20 | async-start | bytes 9437184 | tf_op jit(solution)/shard_map/reduce_scatter | solution.py:307
  1053.3 1174.7 %reduce-scatter.15.cloned.1.call-start = ((), (), s32[]{:S(2)}) async-start(), calls=%async_computation.21 | async-start | bytes 9437184 | tf_op jit(solution)/shard_map/reduce_scatter | solution.py:308
  1064.0 73.4 %copy-start.43 = (f32[8,1,256]{2,1,0:T(1,128)S(1)}, f32[8,1,256]{2,1,0:T(1,128)}, u32[]{:S(2)}) copy-start(f32[8,1,256]{2,1,0:T(1,128)} %copy-done.42) | copy-start | bytes 24580
  1064.0 73.4 %copy-start.45 = (f32[1024]{0:T(1024)S(1)}, f32[1024]{0:T(1024)}, u32[]{:S(2)}) copy-start(f32[1024]{0:T(1024)} %copy-done.44) | copy-start | bytes 12292
  1064.0 73.4 %copy-start.47 = (f32[1024]{0:T(1024)S(1)}, f32[1024]{0:T(1024)}, u32[]{:S(2)}) copy-start(f32[1024]{0:T(1024)} %copy-done.46) | copy-start | bytes 12292
  1137.3 6.2 copy-start.48
  1137.3 6.2 copy-start.49
  1185.6 8.5 copy-start.2
  1185.6 8.5 copy-start.7
  (23 other events, 37.7 us)
Sparse Core Ops, SparseCore 0:
  10.1 52.0 all-gather.16
  64.3 47.5 all-gather.18
  114.1 71.3 all-gather.14
  187.4 71.3 all-gather.12
  260.6 73.1 all-gather.20
  345.0 151.0 all-reduce.9
  498.2 72.9 all-gather.22
  573.3 71.3 all-gather.24
  646.7 73.1 all-gather.26
  744.4 151.0 all-reduce.11
  984.3 153.0 all-reduce.13
  1141.4 88.9 reduce-scatter.10
  1234.6 87.9 reduce-scatter.8
  1326.6 147.0 reduce-scatter.18
  1477.8 146.5 reduce-scatter.20
  1628.5 146.9 reduce-scatter.22
  1779.5 146.9 reduce-scatter.16
  1930.6 146.5 reduce-scatter.12
  2081.4 146.5 reduce-scatter.14
where the time goes:
time: 2240 us; the launch traced here: 2230 us
  waiting for transfers between devices  1760 us (79%)
  matrix products  227 us (10%)
  blocking collectives  113 us (5%)
  other arithmetic  76.6 us (3%)
  local copies, waits for them, and re-layouts  38.1 us (2%)
    dot_general x24, matrix products, dense(): return jnp.dot(left, right, preferred_element_type=jnp.float32)  205 us
    reduce_scatter x1, waiting for transfers between devices, local(): lax.psum_scatter(grad_ffgate, 'dp', scatter_dimension=0, tiled=True)  151 us
    reduce_scatter x1, waiting for transfers between devices, local(): lax.psum_scatter(grad_out, 'dp', scatter_dimension=1, tiled=True)  151 us
    reduce_scatter x1, waiting for transfers between devices, local(): lax.psum_scatter(grad_down, 'dp', scatter_dimension=1, tiled=True)  151 us
    reduce_scatter x1, waiting for transfers between devices, local(): lax.psum_scatter(grad_gate, 'dp', scatter_dimension=0, tiled=True)  151 us
    reduce_scatter x1, waiting for transfers between devices, local(): lax.psum_scatter(grad_value, 'dp', scatter_dimension=0, tiled=True)  151 us
    reduce_scatter x1, waiting for transfers between devices, local(): lax.psum_scatter(grad_ffup, 'dp', scatter_dimension=0, tiled=True)  151 us
    psum x1, waiting for transfers between devices, local(): lax.psum(dense(grad_ffgate_in, back_ffgate.T) + dense(grad_ffup_in, back_...  142 us
  transfers between devices with their start and end apart: 19, of which 18 were waited for; matrix products, arithmetic and copies ran while one was open for 9% of the time, Pallas kernels for 0%

commit v1 on v0

--- a/solution.py
+++ b/solution.py
@@ -203,7 +203,8 @@
     sigmoid_gate = jax.nn.sigmoid(gate)
     swish = gate * sigmoid_gate
     gated = (swish * grouped_flat).astype(jnp.bfloat16)
-    attention = lax.psum(dense(gated, full_out), "tensor")
+    local_x = dense(gated, full_out)
+    attention = jnp.sum(lax.all_gather(local_x, "tensor"), axis=0)
     middle = inputs + attention
     normed_two, scale_two = norm_parts(middle, EPSILON)
     second_in = (normed_two * gain_two.astype(jnp.float32) + shift_two.astype(jnp.float32)).astype(

time: 2240 us -> 2290 us (1.022)
  waiting for transfers between devices: 1760 us -> 1790 us
    all_gather x0 -> x1, waiting for transfers between devices: none -> 163 us  [local(): attention = jnp.sum(lax.all_gather(local_x, 'tensor'), axis=0)]
    psum x1 -> x0, waiting for transfers between devices: 114 us -> none  [local(): attention = lax.psum(dense(gated, full_out), 'tensor')]
  transfers between devices with their start and end apart: 19 -> 19, of which waited for: 18 -> 18; matrix products, arithmetic and copies ran while one was open for 9% -> 10% of each run, Pallas kernels for 0% -> 0%
where the time goes in v1:
time: 2290 us; the launch traced here: 2280 us
  waiting for transfers between devices  1790 us (78%)
  matrix products  227 us (10%)
  blocking collectives  113 us (5%)
  other arithmetic  92.8 us (4%)
  local copies, waits for them, and re-layouts  38.2 us (2%)
    dot_general x24, matrix products, dense(): return jnp.dot(left, right, preferred_element_type=jnp.float32)  205 us
    all_gather x1, waiting for transfers between devices, local(): attention = jnp.sum(lax.all_gather(local_x, 'tensor'), axis=0)  163 us
    reduce_scatter x1, waiting for transfers between devices, local(): lax.psum_scatter(grad_ffgate, 'dp', scatter_dimension=0, tiled=True)  151 us
    reduce_scatter x1, waiting for transfers between devices, local(): lax.psum_scatter(grad_out, 'dp', scatter_dimension=1, tiled=True)  151 us
    reduce_scatter x1, waiting for transfers between devices, local(): lax.psum_scatter(grad_down, 'dp', scatter_dimension=1, tiled=True)  151 us
    reduce_scatter x1, waiting for transfers between devices, local(): lax.psum_scatter(grad_gate, 'dp', scatter_dimension=0, tiled=True)  151 us
    reduce_scatter x1, waiting for transfers between devices, local(): lax.psum_scatter(grad_value, 'dp', scatter_dimension=0, tiled=True)  151 us
    reduce_scatter x1, waiting for transfers between devices, local(): lax.psum_scatter(grad_ffup, 'dp', scatter_dimension=0, tiled=True)  151 us
  transfers between devices with their start and end apart: 19, of which 18 were waited for; matrix products, arithmetic and copies ran while one was open for 10% of the time, Pallas kernels for 0%

profile of v1, /device:TPU:0, one launch (start us, length us, event | category | flops | bytes accessed | tf_op | source)
XLA Modules:
  0.0 2283.1 jit_solution(3459970912912741712)
XLA Ops:
  12.3 3.2 convert_reduce_fusion.1
  19.0 22.3 all-gather.1
  41.4 16.7 all-gather.2
  61.8 3.3 fusion.8
  65.2 5.2 fusion.59
  76.1 35.8 %all-gather.21.cloned.1.call-done = bf16[2048,512]{1,0:T(8,128)(2,1)} async-done(((bf16[256,512]{1,0:T(8,128)(2,1)}), bf16[2048,512]{1,0:T(8,128)(2,1)}) %all-gather.21.cloned.1.call-update) | async-done | bytes 2097168 | tf_op jit(solution)/shard_map/all_gather | solution.py:152
  111.9 5.2 fusion.60
  118.7 2.6 copy.126
  124.0 2.7 multiply_convert_fusion.9
  126.9 2.6 multiply_convert_fusion.6
  129.5 2.6 multiply_convert_fusion.7
  132.2 53.2 %all-gather.17.cloned.1.call-done = bf16[2048,1024]{1,0:T(8,128)(2,1)} async-done(((bf16[256,1024]{1,0:T(8,128)(2,1)}), bf16[2048,1024]{1,0:T(8,128)(2,1)}) %all-gather.17.cloned.1.call-update) | async-done | bytes 4194320 | tf_op jit(solution)/shard_map/all_gather | solution.py:153
  185.4 8.6 convolution_convert_fusion.1
  199.2 59.6 %all-gather.15.cloned.1.call-done = bf16[2048,1024]{1,0:T(8,128)(2,1)} async-done(((bf16[256,1024]{1,0:T(8,128)(2,1)}), bf16[2048,1024]{1,0:T(8,128)(2,1)}) %all-gather.15.cloned.1.call-update) | async-done | bytes 4194320 | tf_op jit(solution)/shard_map/all_gather | solution.py:154
  258.8 12.3 multiply_convert_fusion.5
  271.0 62.8 %all-gather.23.cloned.1.call-done = bf16[1024,2048]{1,0:T(8,128)(2,1)} async-done(((bf16[1024,256]{1,0:T(8,128)(2,1)}), bf16[1024,2048]{1,0:T(8,128)(2,1)}) %all-gather.23.cloned.1.call-update) | async-done | bytes 4194320 | tf_op jit(solution)/shard_map/all_gather | solution.py:155
  333.9 11.0 fusion.63
  347.2 17.7 all-gather.3
  365.0 16.8 all-gather.4
  381.8 162.9 %all-gather.31.cloned.1.call-done = f32[4096,2048]{1,0:T(8,128)} async-done(((f32[1024,2048]{1,0:T(8,128)}), f32[4096,2048]{1,0:T(8,128)}) %all-gather.31.cloned.1.call-update) | async-done | bytes 33554448 | tf_op jit(solution)/shard_map/all_gather | solution.py:207
  544.7 16.4 reduce_sum.157
  561.1 5.5 fusion.55
  570.1 3.0 add_convert_fusion.2
  573.1 46.6 %all-gather.25.cloned.1.call-done = bf16[2048,1024]{1,0:T(8,128)(2,1)} async-done(((bf16[256,1024]{1,0:T(8,128)(2,1)}), bf16[2048,1024]{1,0:T(8,128)(2,1)}) %all-gather.25.cloned.1.call-update) | async-done | bytes 4194320 | tf_op jit(solution)/shard_map/all_gather | solution.py:156
  619.7 10.0 fusion.64
  629.6 63.5 %all-gather.27.cloned.1.call-done = bf16[2048,1024]{1,0:T(8,128)(2,1)} async-done(((bf16[256,1024]{1,0:T(8,128)(2,1)}), bf16[2048,1024]{1,0:T(8,128)(2,1)}) %all-gather.27.cloned.1.call-update) | async-done | bytes 4194320 | tf_op jit(solution)/shard_map/all_gather | solution.py:157
  693.1 10.0 fusion.65
  703.2 65.2 %all-gather.29.cloned.1.call-done = bf16[1024,2048]{1,0:T(8,128)(2,1)} async-done(((bf16[1024,256]{1,0:T(8,128)(2,1)}), bf16[1024,2048]{1,0:T(8,128)(2,1)}) %all-gather.29.cloned.1.call-update) | async-done | bytes 4194320 | tf_op jit(solution)/shard_map/all_gather | solution.py:158
  768.4 12.8 multiply_convert_fusion.3
  781.2 4.6 fusion.66
  785.8 6.9 convolution_add_fusion
  793.0 9.4 convolution_convert_fusion
  802.4 141.5 %all-reduce.9.cloned.1.call-done = f32[1024,2048]{1,0:T(8,128)} async-done(((f32[1024,2048]{1,0:T(8,128)}), f32[1024,2048]{1,0:T(8,128)}) %all-reduce.9.cloned.1.call-update) | async-done | bytes 8388624 | tf_op jit(solution)/shard_map/psum | solution.py:257
  944.0 8.3 multiply_reduce_fusion
  952.3 7.5 multiply_add_fusion
  960.0 13.0 multiply_convert_fusion
  973.0 3.5 bitcast_reduce_fusion
  985.3 3.2 fusion.40
  997.4 2.6 copy.103
  1000.1 4.2 add_convert_fusion.3
  1007.3 6.9 fusion.68
  1014.2 6.9 fusion.69
  1021.0 11.4 add_convert_fusion
  1032.6 6.7 fusion.71
  1040.6 6.5 fusion.70
  1048.8 9.1 fusion.74
  1059.5 9.1 fusion.75
  1070.3 8.8 fusion.76
  1080.8 10.1 fusion.29
  1092.5 9.1 fusion.72
  1103.1 9.1 fusion.73
  1114.1 71.5 %all-reduce.11.cloned.1.call-done = (bf16[1024,2048]{1,0:T(8,128)(2,1)}, bf16[1024,2048]{1,0:T(8,128)(2,1)}) async-done(((bf16[1024,2048]{1,0:T(8,128)(2,1)}, bf16[1024,2048]{1,0:T(8,128)(2,1)}), (bf16[1024,2048]{1,0:T(8,128)(2,1)}, bf16[1024,2048]{1,0:T(8,128)(2,1)})) %all-reduce.11.cloned.1.call-update) | async-done | bytes 8388624 | tf_op jit(solution)/shard_map/psum | solution.py:218
  1185.6 6.2 fusion.14
  1191.9 39.5 %all-reduce.4 = (f32[2048]{0:T(1024)S(1)}, f32[2048]{0:T(1024)S(1)}, f32[2048]{0:T(1024)S(1)}, f32[2048]{0:T(1024)S(1)}) all-reduce(f32[2048]{0:T(1024)S(1)} %get-tuple-element.68, f32[2048]{0:T(1024)S(1)} %get-tuple-element.72, f32[2048]{0:T(1024)S(1)} %copy-done.48, ...), channel_id=11, replica_groups=mesh['dp'=8,'tensor'=4] {'dp'}, use_global_device_ids=true, to_apply=%region_25.26.clone | all-reduce | flops 8192 | bytes 65536
  1233.9 8.5 add_convert_fusion.1
  1242.4 7.4 fusion.11
  1249.8 28.9 %reduce-scatter.11.cloned.1.call-done = f32[256,512]{1,0:T(8,128)} async-done(((f32[2048,512]{1,0:T(8,128)}), f32[256,512]{1,0:T(8,128)}) %reduce-scatter.11.cloned.1.call-update) | async-done | bytes 524304 | tf_op jit(solution)/shard_map/reduce_scatter | solution.py:307
  1278.7 92.2 %reduce-scatter.9.cloned.1.call-done = f32[256,512]{1,0:T(8,128)} async-done(((f32[2048,512]{1,0:T(8,128)}), f32[256,512]{1,0:T(8,128)}) %reduce-scatter.9.cloned.1.call-update) | async-done | bytes 524304 | tf_op jit(solution)/shard_map/reduce_scatter | solution.py:306
  1370.9 151.2 %reduce-scatter.19.cloned.1.call-done = f32[256,1024]{1,0:T(8,128)} async-done(((f32[2048,1024]{1,0:T(8,128)}), f32[256,1024]{1,0:T(8,128)}) %reduce-scatter.19.cloned.1.call-update) | async-done | bytes 1048592 | tf_op jit(solution)/shard_map/reduce_scatter | solution.py:311
  1522.1 150.6 %reduce-scatter.21.cloned.1.call-done = f32[256,1024]{1,0:T(8,128)} async-done(((f32[2048,1024]{1,0:T(8,128)}), f32[256,1024]{1,0:T(8,128)}) %reduce-scatter.21.cloned.1.call-update) | async-done | bytes 1048592 | tf_op jit(solution)/shard_map/reduce_scatter | solution.py:312
  1672.7 151.0 %reduce-scatter.23.cloned.1.call-done = f32[1024,256]{1,0:T(8,128)} async-done(((f32[1024,2048]{1,0:T(8,128)}), f32[1024,256]{1,0:T(8,128)}) %reduce-scatter.23.cloned.1.call-update) | async-done | bytes 1048592 | tf_op jit(solution)/shard_map/reduce_scatter | solution.py:313
  1823.7 151.1 %reduce-scatter.17.cloned.1.call-done = f32[1024,256]{1,0:T(8,128)} async-done(((f32[1024,2048]{1,0:T(8,128)}), f32[1024,256]{1,0:T(8,128)}) %reduce-scatter.17.cloned.1.call-update) | async-done | bytes 1048592 | tf_op jit(solution)/shard_map/reduce_scatter | solution.py:310
  1974.8 150.7 %reduce-scatter.13.cloned.1.call-done = f32[256,1024]{1,0:T(8,128)} async-done(((f32[2048,1024]{1,0:T(8,128)}), f32[256,1024]{1,0:T(8,128)}) %reduce-scatter.13.cloned.1.call-update) | async-done | bytes 1048592 | tf_op jit(solution)/shard_map/reduce_scatter | solution.py:308
  2125.5 150.8 %reduce-scatter.15.cloned.1.call-done = f32[256,1024]{1,0:T(8,128)} async-done(((f32[2048,1024]{1,0:T(8,128)}), f32[256,1024]{1,0:T(8,128)}) %reduce-scatter.15.cloned.1.call-update) | async-done | bytes 1048592 | tf_op jit(solution)/shard_map/reduce_scatter | solution.py:309
  (236 shorter events, 68.8 us)
Async XLA Ops:
  7.2 58.0 %all-gather.19.cloned.1.call-start = ((), (), s32[]{:S(2)}) async-start(), calls=%async_computation.10 | async-start | bytes 2359296 | tf_op jit(solution)/shard_map/all_gather | solution.py:151
  7.9 104.0 %all-gather.21.cloned.1.call-start = ((), (), s32[]{:S(2)}) async-start(), calls=%async_computation.11 | async-start | bytes 2359296 | tf_op jit(solution)/shard_map/all_gather | solution.py:152
  8.7 176.8 %all-gather.17.cloned.1.call-start = ((), (), s32[]{:S(2)}) async-start(), calls=%async_computation.9 | async-start | bytes 4718592 | tf_op jit(solution)/shard_map/all_gather | solution.py:153
  9.4 249.4 %all-gather.15.cloned.1.call-start = ((), (), s32[]{:S(2)}) async-start(), calls=%async_computation.8 | async-start | bytes 4718592 | tf_op jit(solution)/shard_map/all_gather | solution.py:154
  10.0 323.9 %all-gather.23.cloned.1.call-start = ((), (), s32[]{:S(2)}) async-start(), calls=%async_computation.12 | async-start | bytes 4718592 | tf_op jit(solution)/shard_map/all_gather | solution.py:155
  10.6 534.2 %all-gather.31.cloned.1.call-start = ((), (), s32[]{:S(2)}) async-start(), calls=%async_computation.25 | async-start | bytes 41943040 | tf_op jit(solution)/shard_map/all_gather | solution.py:207
  10.6 4.9 copy-start.1
  12.3 4.5 copy-start.50
  12.3 4.5 copy-start.55
  15.5 3.5 copy-start.56
  15.5 25.8 %copy-start.57 = (bf16[256]{0:T(256)(128)(2,1)S(1)}, bf16[256]{0:T(256)(128)(2,1)}, u32[]{:S(2)}) copy-start(bf16[256]{0:T(256)(128)(2,1)} %param.26) | copy-start | bytes 1540
  15.5 46.3 %copy-start.44 = (f32[1024]{0:T(1024)}, f32[1024]{0:T(1024)S(1)}, u32[]{:S(2)}) copy-start(f32[1024]{0:T(1024)S(1)} %broadcast_multiply_fusion.9) | copy-start | bytes 12292
  16.8 45.1 %copy-start.46 = (f32[1024]{0:T(1024)}, f32[1024]{0:T(1024)S(1)}, u32[]{:S(2)}) copy-start(f32[1024]{0:T(1024)S(1)} %add_rsqrt_fusion.2) | copy-start | bytes 12292
  17.0 106.9 %copy-start.14 = (f32[1024,128]{1,0:T(8,128)}, f32[1024,128]{1,0:T(8,128)S(1)}, u32[]{:S(2)}) copy-start(f32[1024,128]{1,0:T(8,128)S(1)} %get-tuple-element.103) | copy-start | bytes 1572868
  17.0 106.9 %copy-start.16 = (f32[1024,128]{1,0:T(8,128)}, f32[1024,128]{1,0:T(8,128)S(1)}, u32[]{:S(2)}) copy-start(f32[1024,128]{1,0:T(8,128)S(1)} %get-tuple-element.104) | copy-start | bytes 1572868
  19.0 105.0 %copy-start.18 = (f32[1024,128]{1,0:T(8,128)}, f32[1024,128]{1,0:T(8,128)S(1)}, u32[]{:S(2)}) copy-start(f32[1024,128]{1,0:T(8,128)S(1)} %get-tuple-element.105) | copy-start | bytes 1572868
  19.0 105.0 %copy-start.20 = (f32[1024,128]{1,0:T(8,128)}, f32[1024,128]{1,0:T(8,128)S(1)}, u32[]{:S(2)}) copy-start(f32[1024,128]{1,0:T(8,128)S(1)} %get-tuple-element.106) | copy-start | bytes 1572868
  41.3 20.5 copy-start.42
  123.9 2.9 copy-start.28
  124.0 2.9 copy-start.38
  126.7 2.9 copy-start.10
  126.7 2.9 copy-start.12
  126.9 2.7 copy-start.30
  126.9 2.7 copy-start.40
  185.4 8.6 copy-start.26
  194.0 3.7 copy-start.60
  344.8 20.1 copy-start.59
  344.9 274.8 %all-gather.25.cloned.1.call-start = ((), (), s32[]{:S(2)}) async-start(), calls=%async_computation.13 | async-start | bytes 4718592 | tf_op jit(solution)/shard_map/all_gather | solution.py:156
  345.6 347.5 %all-gather.27.cloned.1.call-start = ((), (), s32[]{:S(2)}) async-start(), calls=%async_computation.14 | async-start | bytes 4718592 | tf_op jit(solution)/shard_map/all_gather | solution.py:157
  346.4 422.0 %all-gather.29.cloned.1.call-start = ((), (), s32[]{:S(2)}) async-start(), calls=%async_computation.15 | async-start | bytes 4718592 | tf_op jit(solution)/shard_map/all_gather | solution.py:158
  347.1 596.9 %all-reduce.9.cloned.1.call-start = ((), (), s32[]{:S(2)}) async-start(), calls=%async_computation.16 | async-start | bytes 16777216 | tf_op jit(solution)/shard_map/psum | solution.py:257
  566.7 3.4 copy-start
  768.4 12.8 copy-start.52
  781.2 4.6 copy-start.66
  781.2 4.6 copy-start.64
  781.2 4.6 copy-start.53
  792.8 392.8 %all-reduce.11.cloned.1.call-start = ((), (), s32[]{:S(2)}) async-start(), calls=%async_computation.26 | async-start | bytes 16777216 | tf_op jit(solution)/shard_map/psum | solution.py:218
  944.0 8.3 copy-start.23
  952.3 7.5 copy-start.5
  952.3 7.7 copy-start.6
  959.8 13.2 copy-start.3
  978.9 6.4 copy-start.8
  992.5 7.6 copy-start.9
  1000.1 4.3 copy-start.36
  1000.1 4.3 copy-start.54
  1004.3 2.4 copy-start.33
  1004.3 2.9 copy-start.51
  1007.3 6.9 copy-start.22
  1007.3 6.9 copy-start.24
  1032.4 246.3 %reduce-scatter.11.cloned.1.call-start = ((), (), s32[]{:S(2)}) async-start(), calls=%async_computation.18 | async-start | bytes 4718592 | tf_op jit(solution)/shard_map/reduce_scatter | solution.py:307
  1039.4 331.5 %reduce-scatter.9.cloned.1.call-start = ((), (), s32[]{:S(2)}) async-start(), calls=%async_computation.17 | async-start | bytes 4718592 | tf_op jit(solution)/shard_map/reduce_scatter | solution.py:306
  1047.1 474.9 %reduce-scatter.19.cloned.1.call-start = ((), (), s32[]{:S(2)}) async-start(), calls=%async_computation.22 | async-start | bytes 9437184 | tf_op jit(solution)/shard_map/reduce_scatter | solution.py:311
  1057.9 614.8 %reduce-scatter.21.cloned.1.call-start = ((), (), s32[]{:S(2)}) async-start(), calls=%async_computation.23 | async-start | bytes 9437184 | tf_op jit(solution)/shard_map/reduce_scatter | solution.py:312
  1068.7 755.1 %reduce-scatter.23.cloned.1.call-start = ((), (), s32[]{:S(2)}) async-start(), calls=%async_computation.24 | async-start | bytes 9437184 | tf_op jit(solution)/shard_map/reduce_scatter | solution.py:313
  1079.2 895.6 %reduce-scatter.17.cloned.1.call-start = ((), (), s32[]{:S(2)}) async-start(), calls=%async_computation.21 | async-start | bytes 9437184 | tf_op jit(solution)/shard_map/reduce_scatter | solution.py:310
  1090.9 1034.6 %reduce-scatter.13.cloned.1.call-start = ((), (), s32[]{:S(2)}) async-start(), calls=%async_computation.19 | async-start | bytes 9437184 | tf_op jit(solution)/shard_map/reduce_scatter | solution.py:308
  1101.6 1174.7 %reduce-scatter.15.cloned.1.call-start = ((), (), s32[]{:S(2)}) async-start(), calls=%async_computation.20 | async-start | bytes 9437184 | tf_op jit(solution)/shard_map/reduce_scatter | solution.py:309
  1112.2 73.4 %copy-start.43 = (f32[8,1,256]{2,1,0:T(1,128)S(1)}, f32[8,1,256]{2,1,0:T(1,128)}, u32[]{:S(2)}) copy-start(f32[8,1,256]{2,1,0:T(1,128)} %copy-done.42) | copy-start | bytes 24580
  1112.2 73.4 %copy-start.45 = (f32[1024]{0:T(1024)S(1)}, f32[1024]{0:T(1024)}, u32[]{:S(2)}) copy-start(f32[1024]{0:T(1024)} %copy-done.44) | copy-start | bytes 12292
  1112.2 73.4 %copy-start.47 = (f32[1024]{0:T(1024)S(1)}, f32[1024]{0:T(1024)}, u32[]{:S(2)}) copy-start(f32[1024]{0:T(1024)} %copy-done.46) | copy-start | bytes 12292
  1185.6 6.2 copy-start.48
  1185.6 6.2 copy-start.49
  1233.9 8.5 copy-start.2
  1233.9 8.5 copy-start.7
  (23 other events, 37.8 us)
Sparse Core Ops, SparseCore 0:
  10.1 52.0 all-gather.18
  64.3 47.5 all-gather.20
  114.1 71.3 all-gather.16
  187.4 71.3 all-gather.14
  260.6 73.1 all-gather.22
  345.0 199.6 all-gather.30
  546.8 72.7 all-gather.24
  621.8 71.3 all-gather.26
  695.2 73.1 all-gather.28
  792.9 151.0 all-reduce.8
  1032.5 153.0 all-reduce.10
  1189.7 88.9 reduce-scatter.10
  1282.9 87.9 reduce-scatter.8
  1374.9 147.0 reduce-scatter.18
  1526.1 146.5 reduce-scatter.20
  1676.8 146.9 reduce-scatter.22
  1827.8 146.9 reduce-scatter.16
  1978.9 146.5 reduce-scatter.12
  2129.7 146.5 reduce-scatter.14
